TPU v7x, 32 devices: a whole 2x2x4 slice. The times are simulated.
32 devices in a mesh: dom: 4 (over z), shard: 8 (over y, x, core).
Axes of the slice: x: 2, y: 2, z: 4, core: 2. Of those that a mesh axis runs over, the one named last changes fastest.
Arguments:
- features: bfloat16 [131072, 1024], P(('dom', 'shard')), may hold values from -6 to 6
- enc_weight: bfloat16 [1024, 512], replicated, may hold values from -0.1875 to 0.1875
- pack_index: int32 [4, 8, 8, 512], P('dom', 'shard'), may hold values from 0 to 4095, as said below
- place_index: int32 [4, 8, 4096], P('dom', 'shard'), may hold values from 0 to 4095, as said below
- halo_send_one: int32 [4, 8, 4, 8, 16], P('dom', 'shard'), may hold values from 0 to 4096, as said below
- halo_send_two: int32 [4, 8, 4, 8, 16], P('dom', 'shard'), may hold values from 0 to 4096, as said below
- tile_index_one: int32 [1024, 6], P(('dom', 'shard')), may hold values from 0 to 35
- tile_index_two: int32 [1024, 6], P(('dom', 'shard')), may hold values from 0 to 35
- tile_live_one: int32 [1024], P(('dom', 'shard')), may hold values from 1 to 6, as said below
- tile_live_two: int32 [1024], P(('dom', 'shard')), may hold values from 1 to 6, as said below
- tiles_one: bfloat16 [1024, 6, 128, 128], P(('dom', 'shard')), may hold values from 0 to 2, as said below
- tiles_two: bfloat16 [1024, 6, 128, 128], P(('dom', 'shard')), may hold values from 0 to 2, as said below
- degree: int32 [131072], P(('dom', 'shard')), may hold values from 32 to 255
- self_weight_one: bfloat16 [512, 512], replicated, may hold values from -0.25 to 0.25
- neigh_weight_one: bfloat16 [512, 512], replicated, may hold values from -0.25 to 0.25
- self_weight_two: bfloat16 [512, 512], replicated, may hold values from -0.25 to 0.25
- neigh_weight_two: bfloat16 [512, 512], replicated, may hold values from -0.25 to 0.25
- head_weight: bfloat16 [512], replicated, may hold values from -0.25 to 0.25
Outputs:
- embedding: bfloat16 [131072, 512], P(('dom', 'shard'))
- probability: float32 [131072], P(('dom', 'shard'))
Inputs may be any that keep to these rules, and one draw needn't show every extreme that they name: pack_index[d, s, t, :] lists the 512 hash-order rows that device s of group d sends to owner t; every local row is sent exactly once. place_index[d, t, :] is a permutation of the slots that owner t receives. halo_send_one[d, s, d2, s2, :] lists rows of device (d, s) for device (d2, s2), then 4096 in empty slots; a device sends nothing to itself, exactly 16 rows to one device and 1 to 16 rows to every other. `halo_send_two`: as halo_send_one. `tile_live_one`: every device has a block with all 6 slots live. `tile_live_two`: every device has a block with all 6 slots live. `tiles_one`: nonnegative edge weights. `tiles_two`: nonnegative edge weights.
All inputs are finite; a program needn't handle non-finite values.
Results may differ from a plain program's by a relative error of at most 0.0054.
Values may be sent and summed in bfloat16 or wider, within the bound.
A program may use at most 192 MiB of HBM per device.

v0:
```python
import jax
import jax.numpy as jnp
from jax import lax
from jax.sharding import PartitionSpec as P


def sage_layer(
    hidden_in, halo_send, tile_index, tile_live, tiles, degree, self_weight, neigh_weight
):
    row_count, width = hidden_in.shape
    groups = lax.axis_size("dom")
    group_size = lax.axis_size("shard")
    bound_cap = halo_send.shape[-1]
    padded = jnp.concatenate([hidden_in, jnp.zeros((1, width), jnp.bfloat16)], axis=0)
    outgoing = padded[halo_send.reshape(-1)].reshape(groups, group_size, bound_cap, width)
    arrived = lax.all_to_all(
        outgoing.reshape(groups * group_size, bound_cap, width),
        ("dom", "shard"),
        split_axis=0,
        concat_axis=0,
        tiled=True,
    )
    tile_size = tiles.shape[-1]
    sources = jnp.concatenate([hidden_in, arrived.reshape(-1, width)], axis=0).reshape(
        -1, tile_size, width
    )
    slot_live = jnp.arange(tiles.shape[1], dtype=jnp.int32)[None, :] < tile_live[:, None]
    masked = jnp.where(slot_live[:, :, None, None], tiles, jnp.zeros((), jnp.bfloat16))
    picked = sources[tile_index]
    summed = jnp.einsum(
        "bkij,bkjf->bif", masked, picked, preferred_element_type=jnp.float32
    ).reshape(row_count, width)
    aggregate = (summed / degree[:, None].astype(jnp.float32)).astype(jnp.bfloat16)
    mixed = jnp.dot(hidden_in, self_weight, preferred_element_type=jnp.float32) + jnp.dot(
        aggregate, neigh_weight, preferred_element_type=jnp.float32
    )
    active = jnp.maximum(mixed, 0.0)
    scaled = active * lax.rsqrt(jnp.mean(active * active, axis=-1, keepdims=True) + 1e-06)
    return scaled.astype(jnp.bfloat16)


def per_device(
    features,
    enc_weight,
    pack_index,
    place_index,
    halo_send_one,
    halo_send_two,
    tile_index_one,
    tile_index_two,
    tile_live_one,
    tile_live_two,
    tiles_one,
    tiles_two,
    degree,
    self_weight_one,
    neigh_weight_one,
    self_weight_two,
    neigh_weight_two,
    head_weight,
):
    group_size = lax.axis_size("shard")
    width = enc_weight.shape[1]
    packing = pack_index.reshape(-1)
    encoded = jnp.maximum(
        jnp.dot(features, enc_weight, preferred_element_type=jnp.float32), 0.0
    ).astype(jnp.bfloat16)
    outgoing = encoded[packing].reshape(group_size, -1, width)
    arrived = lax.all_to_all(outgoing, "shard", split_axis=0, concat_axis=0, tiled=True)
    owned = arrived.reshape(-1, width)[place_index.reshape(-1)]
    layer_one = sage_layer(
        owned,
        halo_send_one,
        tile_index_one,
        tile_live_one,
        tiles_one,
        degree,
        self_weight_one,
        neigh_weight_one,
    )
    embedding = sage_layer(
        layer_one,
        halo_send_two,
        tile_index_two,
        tile_live_two,
        tiles_two,
        degree,
        self_weight_two,
        neigh_weight_two,
    )
    probability = jax.nn.sigmoid(
        jnp.dot(embedding, head_weight, preferred_element_type=jnp.float32)
    )
    return (embedding, probability)


def solution(mesh):
    placed = (
        P(("dom", "shard"), None),
        P(),
        P("dom", "shard", None, None),
        P("dom", "shard", None),
        P("dom", "shard", None, None, None),
        P("dom", "shard", None, None, None),
        P(("dom", "shard"), None),
        P(("dom", "shard"), None),
        P(("dom", "shard")),
        P(("dom", "shard")),
        P(("dom", "shard"), None, None, None),
        P(("dom", "shard"), None, None, None),
        P(("dom", "shard")),
        P(),
        P(),
        P(),
        P(),
        P(),
    )
    return jax.shard_map(
        per_device,
        mesh=mesh,
        in_specs=placed,
        out_specs=(P(("dom", "shard"), None), P(("dom", "shard"))),
        check_vma=False,
    )
```

profile of v0, /device:TPU:0, one launch (start us, length us, event | category | flops | bytes accessed | tf_op | source)
XLA Modules:
  0.0 256.0 jit_solution(2594721250184634413)
XLA Ops:
  1.9 9.4 %maximum_convert_fusion = bf16[4096,512]{1,0:T(8,128)(2,1)} fusion(bf16[4096,1024]{1,0:T(8,128)(2,1)} %param.18, bf16[1024,512]{1,0:T(8,128)(2,1)S(1)} %copy-done), kind=kOutput, calls=%fused_computation.16 | convolution fusion | flops 4299161600 | bytes 13631488 | tf_op jit(solution)/shard_map/dot_general | solution.py:66
  11.3 20.2 %gather_fusion = bf16[4096,512]{1,0:T(8,128)(2,1)} fusion(bf16[4096,512]{1,0:T(8,128)(2,1)} %maximum_convert_fusion, s32[4096]{0:T(1024)S(1)} %broadcast_clamp_fusion.1), kind=kCustom, calls=%fused_computation | custom fusion | bytes 8404992 | tf_op jit(solution)/shard_map/gather | solution.py:68
  31.5 5.3 %all-to-all-start = ((bf16[8,512,512]{2,1,0:T(8,128)(2,1)}), bf16[8,512,512]{2,1,0:T(8,128)(2,1)}, u32[]{:S(2)}, u32[]{:S(2)}) async-start(bf16[8,512,512]{2,1,0:T(8,128)(2,1)} %bitcast.57), calls=%async_computation | async-start | bytes 8388608 | tf_op jit(solution)/shard_map/all_to_all | solution.py:69
  37.0 49.0 %all-to-all-done = bf16[8,512,512]{2,1,0:T(8,128)(2,1)} async-done(((bf16[8,512,512]{2,1,0:T(8,128)(2,1)}), bf16[8,512,512]{2,1,0:T(8,128)(2,1)}, u32[]{:S(2)}, u32[]{:S(2)}) %all-to-all-start) | async-done | bytes 4194336 | tf_op jit(solution)/shard_map/all_to_all | solution.py:69
  86.0 20.2 %gather_fusion.1 = bf16[4096,512]{1,0:T(8,128)(2,1)} fusion(bf16[4096,512]{1,0:T(8,128)(2,1)} %bitcast.2, s32[4096]{0:T(1024)S(1)} %broadcast_clamp_fusion), kind=kCustom, calls=%fused_computation.1 | custom fusion | bytes 8404992 | tf_op jit(solution)/shard_map/gather | solution.py:70
  106.2 4.5 %concatenate.12 = bf16[4097,512]{1,0:T(8,128)(2,1)} pad(bf16[4096,512]{1,0:T(8,128)(2,1)} %gather_fusion.1, bf16[]{:T(256)} %constant.12.clone.1), padding=0_1x0_0 | pad | bytes 8389634 | tf_op jit(solution)/shard_map/concatenate | solution.py:14
  110.7 5.4 %gather_fusion.2 = bf16[512,512]{1,0:T(8,128)(2,1)} fusion(bf16[4097,512]{1,0:T(8,128)(2,1)} %concatenate.12, s32[1024]{0:T(1024)S(1)} %pad_clamp_fusion.3), kind=kCustom, calls=%fused_computation.2 | custom fusion | bytes 1050624 | tf_op jit(solution)/shard_map/gather | solution.py:15
  116.1 4.9 %all-to-all-start.1 = ((bf16[32,16,512]{2,1,0:T(8,128)(2,1)}), bf16[32,16,512]{2,1,0:T(8,128)(2,1)S(1)}, u32[]{:S(2)}, u32[]{:S(2)}) async-start(bf16[32,16,512]{2,1,0:T(8,128)(2,1)} %bitcast.6), calls=%async_computation.1 | async-start | bytes 1048576 | tf_op jit(solution)/shard_map/all_to_all | solution.py:16
  121.3 7.8 %fusion.12 = f32[4096,512]{1,0:T(8,128)} fusion(bf16[4096,512]{1,0:T(8,128)(2,1)} %gather_fusion.1, bf16[512,512]{1,0:T(8,128)(2,1)S(1)} %copy-done.6), kind=kOutput, calls=%fused_computation.46 | convolution fusion | flops 2147483648 | bytes 13107200 | tf_op jit(solution)/shard_map/dot_general | solution.py:34
  129.1 7.3 %all-to-all-done.1 = bf16[32,16,512]{2,1,0:T(8,128)(2,1)S(1)} async-done(((bf16[32,16,512]{2,1,0:T(8,128)(2,1)}), bf16[32,16,512]{2,1,0:T(8,128)(2,1)S(1)}, u32[]{:S(2)}, u32[]{:S(2)}) %all-to-all-start.1) | async-done | bytes 524320 | tf_op jit(solution)/shard_map/all_to_all | solution.py:16
  136.3 4.7 %pad_maximum_fusion = bf16[4608,512]{1,0:T(8,128)(2,1)} fusion(bf16[512,512]{1,0:T(8,128)(2,1)S(1)} %bitcast.58, bf16[4096,512]{1,0:T(8,128)(2,1)} %gather_fusion.1), kind=kLoop, calls=%fused_computation.23 | loop fusion | flops 9437184 | bytes 9437184 | tf_op jit(solution)/shard_map/concatenate | solution.py:24
  141.1 13.5 %gather_fusion.3 = bf16[192,128,512]{2,1,0:T(8,128)(2,1)} fusion(bf16[36,128,512]{2,1,0:T(8,128)(2,1)} %bitcast.53, s32[1024]{0:T(1024)S(1)} %pad_clamp_fusion.2), kind=kCustom, calls=%fused_computation.3 | custom fusion | bytes 50332416 | tf_op jit(solution)/shard_map/gather | solution.py:29
  154.5 15.4 %fusion.4 = f32[32,128,512,1]{2,1,3,0:T(8,128)} fusion(bf16[32,6,128,512]{3,2,1,0:T(8,128)(2,1)} %bitcast.55, bf16[32,6,128,128]{3,2,1,0:T(8,128)(2,1)} %param.28, pred[32,6]{1,0:T(8,128)(4,1)S(1)} %iota_compare_fusion.1), kind=kOutput, calls=%fused_computation.19 | convolution fusion | flops 3224371200 | bytes 39846080 | tf_op jit(solution)/shard_map/bkij,bkjf->bif/dot_general | solution.py:30
  170.0 3.9 %fusion.1 = bf16[4096,512]{1,0:T(8,128)(2,1)S(1)} fusion(f32[32,128,512,1]{2,1,3,0:T(8,128)} %fusion.4, f32[4096]{0:T(1024)S(1)} %convert_element_type.21), kind=kLoop, calls=%fused_computation.9 | loop fusion | flops 4194304 | bytes 12599296 | tf_op jit(solution)/shard_map/convert_element_type | solution.py:33
  173.9 6.4 %multiply_reduce_fusion.1 = (f32[4096]{0:T(1024)S(1)}, f32[4096,512]{1,0:T(8,128)S(1)}) fusion(f32[4096,512]{1,0:T(8,128)} %fusion.12, bf16[4096,512]{1,0:T(8,128)(2,1)S(1)} %fusion.1, bf16[512,512]{1,0:T(8,128)(2,1)S(1)} %copy-done.4), kind=kOutput, calls=%fused_computation.14 | convolution fusion | flops 2155868160 | bytes 21512192 | tf_op jit(solution)/shard_map/dot_general | solution.py:34
  185.3 5.4 %gather_fusion.4 = bf16[512,512]{1,0:T(8,128)(2,1)} fusion(bf16[4097,512]{1,0:T(8,128)(2,1)} %concatenate.14, s32[1024]{0:T(1024)S(1)} %pad_clamp_fusion.1), kind=kCustom, calls=%fused_computation.4 | custom fusion | bytes 1050624 | tf_op jit(solution)/shard_map/gather | solution.py:15
  190.7 3.3 %all-to-all-start.2 = ((bf16[32,16,512]{2,1,0:T(8,128)(2,1)}), bf16[32,16,512]{2,1,0:T(8,128)(2,1)S(1)}, u32[]{:S(2)}, u32[]{:S(2)}) async-start(bf16[32,16,512]{2,1,0:T(8,128)(2,1)} %bitcast.14), calls=%async_computation.2 | async-start | bytes 1048576 | tf_op jit(solution)/shard_map/all_to_all | solution.py:16
  194.3 7.8 %fusion.13 = f32[4096,512]{1,0:T(8,128)} fusion(bf16[4096,512]{1,0:T(8,128)(2,1)} %copy-done.2, bf16[512,512]{1,0:T(8,128)(2,1)S(1)} %copy-done.7), kind=kOutput, calls=%fused_computation.47 | convolution fusion | flops 2147483648 | bytes 13107200 | tf_op jit(solution)/shard_map/dot_general | solution.py:34
  202.1 7.2 %all-to-all-done.2 = bf16[32,16,512]{2,1,0:T(8,128)(2,1)S(1)} async-done(((bf16[32,16,512]{2,1,0:T(8,128)(2,1)}), bf16[32,16,512]{2,1,0:T(8,128)(2,1)S(1)}, u32[]{:S(2)}, u32[]{:S(2)}) %all-to-all-start.2) | async-done | bytes 524320 | tf_op jit(solution)/shard_map/all_to_all | solution.py:16
  209.3 4.7 %pad_maximum_fusion.1 = bf16[4608,512]{1,0:T(8,128)(2,1)} fusion(bf16[512,512]{1,0:T(8,128)(2,1)S(1)} %bitcast.59, bf16[4096,512]{1,0:T(8,128)(2,1)} %copy-done.2), kind=kLoop, calls=%fused_computation.24 | loop fusion | flops 9437184 | bytes 9437184 | tf_op jit(solution)/shard_map/concatenate | solution.py:24
  214.0 13.5 %gather_fusion.5 = bf16[192,128,512]{2,1,0:T(8,128)(2,1)} fusion(bf16[36,128,512]{2,1,0:T(8,128)(2,1)} %bitcast.54, s32[1024]{0:T(1024)S(1)} %pad_clamp_fusion), kind=kCustom, calls=%fused_computation.5 | custom fusion | bytes 50332416 | tf_op jit(solution)/shard_map/gather | solution.py:29
  227.5 15.4 %fusion.2 = f32[32,128,512,1]{2,1,3,0:T(8,128)} fusion(bf16[32,6,128,512]{3,2,1,0:T(8,128)(2,1)} %bitcast.56, bf16[32,6,128,128]{3,2,1,0:T(8,128)(2,1)} %param.29, pred[32,6]{1,0:T(8,128)(4,1)S(1)} %iota_compare_fusion), kind=kOutput, calls=%fused_computation.17 | convolution fusion | flops 3224371200 | bytes 39846080 | tf_op jit(solution)/shard_map/bkij,bkjf->bif/dot_general | solution.py:30
  242.9 3.9 %fusion = bf16[4096,512]{1,0:T(8,128)(2,1)S(1)} fusion(f32[32,128,512,1]{2,1,3,0:T(8,128)} %fusion.2, f32[4096]{0:T(1024)S(1)} %convert_element_type.21), kind=kLoop, calls=%fused_computation.7 | loop fusion | flops 4194304 | bytes 12599296 | tf_op jit(solution)/shard_map/convert_element_type | solution.py:33
  246.9 6.4 %multiply_reduce_fusion = (f32[4096]{0:T(1024)S(1)}, f32[4096,512]{1,0:T(8,128)S(1)}) fusion(f32[4096,512]{1,0:T(8,128)} %fusion.13, bf16[4096,512]{1,0:T(8,128)(2,1)S(1)} %fusion, bf16[512,512]{1,0:T(8,128)(2,1)S(1)} %copy-done.5), kind=kOutput, calls=%fused_computation.11 | convolution fusion | flops 2155868160 | bytes 21512192 | tf_op jit(solution)/shard_map/dot_general | solution.py:34
  (64 shorter events, 9.7 us)
Async XLA Ops:
  0.6 1.2 copy-start
  31.5 5.3 %copy-start.8 = (s32[1,1,4,8,16]{4,3,2,1,0:T(8,128)S(1)}, s32[1,1,4,8,16]{4,3,2,1,0:T(8,128)}, u32[]{:S(2)}) copy-start(s32[1,1,4,8,16]{4,3,2,1,0:T(8,128)} %param.22) | copy-start | bytes 6148
  31.5 5.4 %copy-start.9 = (s32[1,1,4,8,16]{4,3,2,1,0:T(8,128)S(1)}, s32[1,1,4,8,16]{4,3,2,1,0:T(8,128)}, u32[]{:S(2)}) copy-start(s32[1,1,4,8,16]{4,3,2,1,0:T(8,128)} %param.23) | copy-start | bytes 6148
  31.5 5.5 %copy-start.12 = (s32[32,6]{0,1:T(8,128)S(1)}, s32[32,6]{0,1:T(8,128)}, u32[]{:S(2)}) copy-start(s32[32,6]{0,1:T(8,128)} %param.24) | copy-start | bytes 2308
  31.5 5.5 %copy-start.10 = (s32[1,1,4096]{2,1,0:T(1,128)S(1)}, s32[1,1,4096]{2,1,0:T(1,128)}, u32[]{:S(2)}) copy-start(s32[1,1,4096]{2,1,0:T(1,128)} %param.21) | copy-start | bytes 49156
  31.5 54.5 %all-to-all-start = ((bf16[8,512,512]{2,1,0:T(8,128)(2,1)}), bf16[8,512,512]{2,1,0:T(8,128)(2,1)}, u32[]{:S(2)}, u32[]{:S(2)}) async-start(bf16[8,512,512]{2,1,0:T(8,128)(2,1)} %bitcast.57), calls=%async_computation | async-start | bytes 8388608 | tf_op jit(solution)/shard_map/all_to_all | solution.py:69
  106.2 15.0 %copy-start.11 = (s32[4096]{0:T(1024)S(1)}, s32[4096]{0:T(1024)}, u32[]{:S(2)}) copy-start(s32[4096]{0:T(1024)} %param.30) | copy-start | bytes 49156
  106.2 15.1 %copy-start.15 = (s32[32]{0:T(128)S(1)}, s32[32]{0:T(128)}, u32[]{:S(2)}) copy-start(s32[32]{0:T(128)} %param.26) | copy-start | bytes 388
  106.2 15.1 %copy-start.6 = (bf16[512,512]{1,0:T(8,128)(2,1)S(1)}, bf16[512,512]{1,0:T(8,128)(2,1)}, u32[]{:S(2)}) copy-start(bf16[512,512]{1,0:T(8,128)(2,1)} %param.31) | copy-start | bytes 1572868
  116.1 20.3 %all-to-all-start.1 = ((bf16[32,16,512]{2,1,0:T(8,128)(2,1)}), bf16[32,16,512]{2,1,0:T(8,128)(2,1)S(1)}, u32[]{:S(2)}, u32[]{:S(2)}) async-start(bf16[32,16,512]{2,1,0:T(8,128)(2,1)} %bitcast.6), calls=%async_computation.1 | async-start | bytes 1048576 | tf_op jit(solution)/shard_map/all_to_all | solution.py:16
  170.0 3.9 %copy-start.4 = (bf16[512,512]{1,0:T(8,128)(2,1)S(1)}, bf16[512,512]{1,0:T(8,128)(2,1)}, u32[]{:S(2)}) copy-start(bf16[512,512]{1,0:T(8,128)(2,1)} %param.32) | copy-start | bytes 1572868
  181.0 2.0 copy-start.2
  183.1 10.9 %copy-start.13 = (s32[32,6]{0,1:T(8,128)S(1)}, s32[32,6]{0,1:T(8,128)}, u32[]{:S(2)}) copy-start(s32[32,6]{0,1:T(8,128)} %param.25) | copy-start | bytes 2308
  183.1 11.1 %copy-start.14 = (bf16[512]{0:T(512)(128)(2,1)S(1)}, bf16[512]{0:T(512)(128)(2,1)}, u32[]{:S(2)}) copy-start(bf16[512]{0:T(512)(128)(2,1)} %param.35) | copy-start | bytes 3076
  183.1 11.2 %copy-start.16 = (s32[32]{0:T(128)S(1)}, s32[32]{0:T(128)}, u32[]{:S(2)}) copy-start(s32[32]{0:T(128)} %param.27) | copy-start | bytes 388
  183.1 11.3 %copy-start.7 = (bf16[512,512]{1,0:T(8,128)(2,1)S(1)}, bf16[512,512]{1,0:T(8,128)(2,1)}, u32[]{:S(2)}) copy-start(bf16[512,512]{1,0:T(8,128)(2,1)} %param.33) | copy-start | bytes 1572868
  190.7 18.6 %all-to-all-start.2 = ((bf16[32,16,512]{2,1,0:T(8,128)(2,1)}), bf16[32,16,512]{2,1,0:T(8,128)(2,1)S(1)}, u32[]{:S(2)}, u32[]{:S(2)}) async-start(bf16[32,16,512]{2,1,0:T(8,128)(2,1)} %bitcast.14), calls=%async_computation.2 | async-start | bytes 1048576 | tf_op jit(solution)/shard_map/all_to_all | solution.py:16
  242.9 3.9 %copy-start.5 = (bf16[512,512]{1,0:T(8,128)(2,1)S(1)}, bf16[512,512]{1,0:T(8,128)(2,1)}, u32[]{:S(2)}) copy-start(bf16[512,512]{1,0:T(8,128)(2,1)} %param.34) | copy-start | bytes 1572868
  253.3 2.8 %copy-start.1 = (bf16[1024,512]{1,0:T(8,128)(2,1)S(1)}, bf16[1024,512]{1,0:T(8,128)(2,1)}, u32[]{:S(2)}) copy-start(bf16[1024,512]{1,0:T(8,128)(2,1)} %param.19) | copy-start | bytes 3145732
  254.0 2.0 copy-start.3
where the time goes:
time: 257 us; the launch traced here: 256 us
  local copies, waits for them, and re-layouts  88.6 us (34%)
  matrix products  69.8 us (27%)
  waiting for transfers between devices  63.4 us (25%)
  other arithmetic  19.8 us (8%)
  starting transfers between devices  13.5 us (5%)
    all_to_all x1, waiting for transfers between devices, per_device(): lax.all_to_all(outgoing, 'shard', split_axis=0, concat_axis=0, tiled=True)  49 us
    dot_general x2, matrix products, sage_layer(): jnp.einsum('bkij,bkjf->bif', masked, picked, preferred_element_type=jnp.f...  30.9 us
    gather x2, local copies, waits for them, and re-layouts, sage_layer(): picked = sources[tile_index]  26.9 us
    gather x1, local copies, waits for them, and re-layouts, per_device(): owned = arrived.reshape(-1, width)[place_index.reshape(-1)]  20.2 us
    gather x1, local copies, waits for them, and re-layouts, per_device(): outgoing = encoded[packing].reshape(group_size, -1, width)  20.2 us
    dot_general x2, matrix products, sage_layer(): jnp.dot(hidden_in, self_weight, preferred_element_type=jnp.float32)  15.5 us
    all_to_all x2, waiting for transfers between devices, sage_layer(): lax.all_to_all(outgoing.reshape(groups * group_size, bound_cap, width), (...  14.5 us
    dot_general x2, matrix products, sage_layer(): jnp.dot(aggregate, neigh_weight, preferred_element_type=jnp.float32)  12.8 us
  transfers between devices with their start and end apart: 3, of which 3 were waited for; matrix products, arithmetic and copies ran while one was open for 6% of the time, Pallas kernels for 0%

commit v1 on v0

v1 whole, which is shorter than its diff:
```python
import functools

import jax
import jax.numpy as jnp
from jax import lax
from jax.experimental import pallas as pl
from jax.experimental.pallas import tpu as pltpu
from jax.sharding import PartitionSpec as P

LANES = 128
STEP = 512
VMEM_LIMIT = 56 << 20
MESH = pl.DeviceIdType.MESH


def across(ref, ids, rows):
    def body(r, carry):
        row = ref[pl.ds(r, 1), :]
        wide = jnp.broadcast_to(row, (LANES, LANES)).T
        lane = lax.broadcasted_iota(jnp.int32, (LANES, LANES), 1)
        ids[pl.ds(pl.multiple_of(r * LANES, LANES), LANES), :] = wide - lane
        return carry

    lax.fori_loop(0, rows // LANES, body, 0)


def one_hot(ids, first, count):
    return jnp.concatenate(
        [
            jnp.where(ids == first + c * LANES, 1.0, 0.0).astype(jnp.bfloat16)
            for c in range(count // LANES)
        ],
        axis=1,
    )


def dot(a, b):
    return jnp.dot(a, b, preferred_element_type=jnp.float32)


def select_rows(ids, table, acc):
    depth = 2 * STEP
    acc[...] = jnp.zeros_like(acc)

    def body(k, carry):
        base = pl.multiple_of(k * depth, depth)
        acc[...] += dot(one_hot(ids, base, depth), table[pl.ds(base, depth), :])
        return carry

    lax.fori_loop(0, table.shape[0] // depth, body, 0)
    return acc[...].astype(jnp.bfloat16)


def flipped(a, b, n):
    total, bit = 0, 1
    while bit < n:
        p, q = (a // bit) % 2, (b // bit) % 2
        total = total + bit * (p + q - 2 * p * q)
        bit *= 2
    return total


def relay_kernel(
    n,
    features,
    weight,
    packing,
    placing,
    sending,
    owned,
    outgoing,
    feats,
    encoded,
    stage,
    recv,
    pack_ids,
    place_ids,
    send_ids,
    acc,
    sel,
    feat_sem,
    send_sem,
    recv_sem,
):
    rows, width = owned.shape
    cap = rows // n
    dom, me = lax.axis_index("dom"), lax.axis_index("shard")
    parts = rows // STEP

    def chunk(c):
        here = pl.ds(pl.multiple_of(c * STEP, STEP), STEP)
        return pltpu.make_async_copy(features.at[here, :], feats.at[here, :], feat_sem.at[c])

    for c in range(parts):
        chunk(c).start()
    barrier = pltpu.get_barrier_semaphore()

    def greet(m, carry):
        pl.semaphore_signal(
            barrier, inc=1, device_id=(dom, flipped(me, m, n)), device_id_type=MESH
        )
        return carry

    lax.fori_loop(1, n, greet, 0)
    across(packing, pack_ids, rows)
    across(placing, place_ids, rows)
    across(sending, send_ids, outgoing.shape[0])

    def encode(c, carry):
        chunk(c).wait()
        here = pl.ds(pl.multiple_of(c * STEP, STEP), STEP)
        encoded[here, :] = jnp.maximum(dot(feats[here, :], weight[...]), 0.0).astype(jnp.bfloat16)
        return carry

    lax.fori_loop(0, parts, encode, 0)
    pl.semaphore_wait(barrier, n - 1)

    def ids_for(t):
        return pack_ids[pl.ds(pl.multiple_of(t * cap, cap), cap), :]

    def transfer(m):
        return pltpu.make_async_remote_copy(
            src_ref=stage.at[m],
            dst_ref=recv.at[m],
            send_sem=send_sem.at[m],
            recv_sem=recv_sem.at[m],
            device_id=(dom, flipped(me, m, n)),
            device_id_type=MESH,
        )

    def pack(step, carry):
        m = n - step
        stage[m] = select_rows(ids_for(flipped(me, m, n)), encoded, acc)
        transfer(m).start()
        return carry

    lax.fori_loop(1, n, pack, 0)
    stage[0] = select_rows(ids_for(me), encoded, acc)

    def place(source, block, fresh):
        def body(r, carry):
            here = pl.ds(pl.multiple_of(r * STEP, STEP), STEP)
            found = dot(one_hot(place_ids[here, :], source * cap, cap), block[...]).astype(
                jnp.bfloat16
            )
            owned[here, :] = found if fresh else owned[here, :] + found
            return carry

        lax.fori_loop(0, parts, body, 0)

    place(me, stage.at[0], True)

    def arrive(step, carry):
        m = n - step
        transfer(m).wait_recv()
        place(flipped(me, m, n), recv.at[m], False)
        return carry

    lax.fori_loop(1, n, arrive, 0)

    def leave(m, carry):
        transfer(m).wait_send()
        return carry

    lax.fori_loop(1, n, leave, 0)

    def boundary(r, carry):
        here = pl.ds(pl.multiple_of(r * STEP, STEP), STEP)
        outgoing[here, :] = select_rows(send_ids[here, :], owned, sel)
        return carry

    lax.fori_loop(0, outgoing.shape[0] // STEP, boundary, 0)


def relay(features, weight, packing, placing, sending, n):
    rows, depth = features.shape
    width = weight.shape[1]
    cap = rows // n
    count = sending.size
    vmem = pl.BlockSpec(memory_space=pltpu.VMEM)
    flops = 2 * rows * width * (depth + 2 * rows + count)
    return pl.pallas_call(
        functools.partial(relay_kernel, n),
        out_shape=(
            jax.ShapeDtypeStruct((rows, width), jnp.bfloat16),
            jax.ShapeDtypeStruct((count, width), jnp.bfloat16),
        ),
        in_specs=[pl.BlockSpec(memory_space=pl.ANY)] + [vmem] * 4,
        out_specs=(vmem, vmem),
        scratch_shapes=[
            pltpu.VMEM((rows, depth), jnp.bfloat16),
            pltpu.VMEM((rows, width), jnp.bfloat16),
            pltpu.VMEM((n, cap, width), jnp.bfloat16),
            pltpu.VMEM((n, cap, width), jnp.bfloat16),
            pltpu.VMEM((rows, LANES), jnp.int32),
            pltpu.VMEM((rows, LANES), jnp.int32),
            pltpu.VMEM((count, LANES), jnp.int32),
            pltpu.VMEM((cap, width), jnp.float32),
            pltpu.VMEM((STEP, width), jnp.float32),
            pltpu.SemaphoreType.DMA((rows // STEP,)),
            pltpu.SemaphoreType.DMA((n,)),
            pltpu.SemaphoreType.DMA((n,)),
        ],
        compiler_params=pltpu.CompilerParams(
            collective_id=0, has_side_effects=True, vmem_limit_bytes=VMEM_LIMIT
        ),
        cost_estimate=pl.CostEstimate(
            flops=flops, bytes_accessed=rows * depth * 2, transcendentals=0
        ),
    )(
        features,
        weight,
        packing.reshape(-1, LANES),
        placing.reshape(-1, LANES),
        sending.reshape(-1, LANES),
    )


def layer_kernel(
    last,
    index,
    live,
    hidden,
    halo,
    tiles,
    degree,
    self_weight,
    neigh_weight,
    extra,
    out,
    second,
    sources,
    aggregate,
    ids,
    sem,
):
    step = pl.program_id(0)
    rows = hidden.shape[0]
    blocks, slots, size = tiles.shape[:3]

    @pl.when(step == 0)
    def _():
        own = pltpu.make_async_copy(hidden, sources.at[pl.ds(0, rows), :], sem.at[0])
        far = pltpu.make_async_copy(halo, sources.at[pl.ds(rows, halo.shape[0]), :], sem.at[1])
        own.start()
        far.start()
        if not last:
            across(extra, ids, ids.shape[0])
        own.wait()
        far.wait()

    for j in range(blocks):
        block = step * blocks + j
        lit = live[block]
        lhs = jnp.concatenate(
            [
                jnp.where(k < lit, tiles[j, k], jnp.zeros((), jnp.bfloat16))
                for k in range(slots)
            ],
            axis=1,
        )
        rhs = jnp.concatenate(
            [
                sources[pl.ds(pl.multiple_of(index[block * slots + k] * size, size), size), :]
                for k in range(slots)
            ],
            axis=0,
        )
        given = degree[pl.ds(block, 1), :].astype(jnp.float32)
        share = 1.0 / jnp.broadcast_to(given, (LANES, LANES)).T
        total = dot(lhs, rhs)
        aggregate[j * size : (j + 1) * size, :] = (
            total * jnp.concatenate([share] * (total.shape[1] // LANES), axis=1)
        ).astype(jnp.bfloat16)
    span = blocks * size
    own_rows = sources[pl.ds(pl.multiple_of(step * span, span), span), :]
    mixed = dot(own_rows, self_weight[...]) + dot(aggregate[...], neigh_weight[...])
    active = jnp.maximum(mixed, 0.0)
    scale = lax.rsqrt(jnp.mean(active * active, axis=-1, keepdims=True) + 1e-06)
    result = (active * scale).astype(jnp.bfloat16)
    out[...] = result
    if last:
        logits = lax.dot_general(
            extra[...], result, (((1,), (1,)), ((), ())), preferred_element_type=jnp.float32
        )
        second[...] = jax.nn.sigmoid(logits[0:1, :])[None]
    else:

        def boundary(r, carry):
            here = pl.ds(pl.multiple_of(r * STEP, STEP), STEP)
            found = dot(one_hot(ids[here, :], step * span, span), result).astype(jnp.bfloat16)
            second[here, :] = jnp.where(step == 0, jnp.zeros_like(found), second[here, :]) + found
            return carry

        lax.fori_loop(0, second.shape[0] // STEP, boundary, 0)


def sage_layer(
    hidden, halo, tile_index, tile_live, tiles, degree, self_weight, neigh_weight, extra, last
):
    rows, width = hidden.shape
    blocks_all, slots, size = tiles.shape[:3]
    per_step = STEP // size
    steps = blocks_all // per_step
    count = halo.shape[0]
    if last:
        extra = jnp.broadcast_to(extra[None, :], (16, width))
        second_shape = jax.ShapeDtypeStruct((steps, 1, STEP), jnp.float32)
        second_spec = pl.BlockSpec((1, 1, STEP), lambda i, *_: (i, 0, 0))
    else:
        extra = extra.reshape(-1, LANES)
        second_shape = jax.ShapeDtypeStruct((extra.size, width), jnp.bfloat16)
        second_spec = pl.BlockSpec((extra.size, width), lambda i, *_: (0, 0))

    def whole(a):
        return pl.BlockSpec(a.shape, lambda i, *_: (0, 0))

    degree = degree.reshape(-1, LANES)
    any_spec = pl.BlockSpec(memory_space=pl.ANY)
    return pl.pallas_call(
        functools.partial(layer_kernel, last),
        out_shape=(jax.ShapeDtypeStruct((rows, width), jnp.bfloat16), second_shape),
        grid_spec=pltpu.PrefetchScalarGridSpec(
            num_scalar_prefetch=2,
            grid=(steps,),
            in_specs=[
                any_spec,
                any_spec,
                pl.BlockSpec((per_step, slots, size, size), lambda i, *_: (i, 0, 0, 0)),
                whole(degree),
                whole(self_weight),
                whole(neigh_weight),
                whole(extra),
            ],
            out_specs=(pl.BlockSpec((STEP, width), lambda i, *_: (i, 0)), second_spec),
            scratch_shapes=[
                pltpu.VMEM((rows + count, width), jnp.bfloat16),
                pltpu.VMEM((STEP, width), jnp.bfloat16),
                pltpu.VMEM((count, LANES), jnp.int32),
                pltpu.SemaphoreType.DMA((2,)),
            ],
        ),
        compiler_params=pltpu.CompilerParams(vmem_limit_bytes=VMEM_LIMIT),
        cost_estimate=pl.CostEstimate(
            flops=2 * rows * width * (slots * size + 2 * width),
            bytes_accessed=tiles.size * 2 + 4 * rows * width,
            transcendentals=0,
        ),
    )(
        tile_index.reshape(-1),
        tile_live,
        hidden,
        halo,
        tiles,
        degree,
        self_weight,
        neigh_weight,
        extra,
    )


def exchange(outgoing, devices):
    width = outgoing.shape[-1]
    return lax.all_to_all(
        outgoing.reshape(devices, -1, width),
        ("dom", "shard"),
        split_axis=0,
        concat_axis=0,
        tiled=True,
    ).reshape(-1, width)


def per_device(
    features,
    enc_weight,
    pack_index,
    place_index,
    halo_send_one,
    halo_send_two,
    tile_index_one,
    tile_index_two,
    tile_live_one,
    tile_live_two,
    tiles_one,
    tiles_two,
    degree,
    self_weight_one,
    neigh_weight_one,
    self_weight_two,
    neigh_weight_two,
    head_weight,
):
    group_size = lax.axis_size("shard")
    devices = lax.axis_size("dom") * group_size
    owned, outgoing = relay(
        features, enc_weight, pack_index, place_index, halo_send_one, group_size
    )
    layer_one, outgoing = sage_layer(
        owned,
        exchange(outgoing, devices),
        tile_index_one,
        tile_live_one,
        tiles_one,
        degree,
        self_weight_one,
        neigh_weight_one,
        halo_send_two,
        False,
    )
    embedding, probability = sage_layer(
        layer_one,
        exchange(outgoing, devices),
        tile_index_two,
        tile_live_two,
        tiles_two,
        degree,
        self_weight_two,
        neigh_weight_two,
        head_weight,
        True,
    )
    return (embedding, probability.reshape(-1))


def solution(mesh):
    placed = (
        P(("dom", "shard"), None),
        P(),
        P("dom", "shard", None, None),
        P("dom", "shard", None),
        P("dom", "shard", None, None, None),
        P("dom", "shard", None, None, None),
        P(("dom", "shard"), None),
        P(("dom", "shard"), None),
        P(("dom", "shard")),
        P(("dom", "shard")),
        P(("dom", "shard"), None, None, None),
        P(("dom", "shard"), None, None, None),
        P(("dom", "shard")),
        P(),
        P(),
        P(),
        P(),
        P(),
    )
    return jax.shard_map(
        per_device,
        mesh=mesh,
        in_specs=placed,
        out_specs=(P(("dom", "shard"), None), P(("dom", "shard"))),
        check_vma=False,
    )
```

time: 257 us -> 164 us (0.64)
  Pallas kernels: 0 us -> 120 us
  local copies, waits for them, and re-layouts: 88.6 us -> 6.47 us
  matrix products: 69.8 us -> 0 us
  waiting for transfers between devices: 63.4 us -> 28.9 us
  other arithmetic: 19.8 us -> 0 us
  starting transfers between devices: 13.5 us -> 6.99 us
    pallas_call x0 -> x3, Pallas kernels: none -> 120 us  [the longest x1 85.1 us: relay(): pl.pallas_call(functools.partial(relay_kernel, n), out_shape=(jax.ShapeDt...]
    gather x6 -> x0, local copies, waits for them, and re-layouts: 78.1 us -> none  [the longest x2 26.9 us: sage_layer(): picked = sources[tile_index]]
    dot_general x8 -> x0, matrix products: 69.8 us -> none  [the longest x2 30.9 us: sage_layer(): jnp.einsum('bkij,bkjf->bif', masked, picked, preferred_element_type=jnp.f...]
    all_to_all x3 -> x2, waiting for transfers between devices: 63.4 us -> 28.9 us  [exchange(): lax.all_to_all(outgoing.reshape(devices, -1, width), ('dom', 'shard'), sp...]
    concatenate x2 -> x0, other arithmetic: 9.46 us -> none  [sage_layer(): jnp.concatenate([hidden_in, arrived.reshape(-1, width)], axis=0)]
    convert_element_type x5 -> x0, other arithmetic: 9.24 us -> none  [the longest x2 7.8 us: sage_layer(): (summed / degree[:, None].astype(jnp.float32)).astype(jnp.bfloat16)]
    concatenate x2 -> x0, local copies, waits for them, and re-layouts: 6.7 us -> none  [sage_layer(): jnp.concatenate([hidden_in, jnp.zeros((1, width), jnp.bfloat16)], axis=0)]
    all_to_all x3 -> x2, starting transfers between devices: 13.5 us -> 6.99 us  [exchange(): lax.all_to_all(outgoing.reshape(devices, -1, width), ('dom', 'shard'), sp...]
  transfers between devices with their start and end apart: 3 -> 2, of which waited for: 3 -> 2; matrix products, arithmetic and copies ran while one was open for 6% -> 1% of each run, Pallas kernels for 0% -> 0%
where the time goes in v1:
time: 164 us
  Pallas kernels  120 us (73%)
  waiting for transfers between devices  28.9 us (18%)
  starting transfers between devices  6.99 us (4%)
  local copies, waits for them, and re-layouts  6.47 us (4%)
    pallas_call x1, Pallas kernels, relay(): pl.pallas_call(functools.partial(relay_kernel, n), out_shape=(jax.ShapeDt...  85.1 us
    pallas_call x2, Pallas kernels, sage_layer(): pl.pallas_call(functools.partial(layer_kernel, last), out_shape=(jax.Shap...  35.3 us
    all_to_all x2, waiting for transfers between devices, exchange(): lax.all_to_all(outgoing.reshape(devices, -1, width), ('dom', 'shard'), sp...  28.9 us
    all_to_all x2, starting transfers between devices, exchange(): lax.all_to_all(outgoing.reshape(devices, -1, width), ('dom', 'shard'), sp...  6.99 us
  transfers between devices with their start and end apart: 2, of which 2 were waited for; matrix products, arithmetic and copies ran while one was open for 1% of the time, Pallas kernels for 0%

profile of v1, /device:TPU:0, one launch (start us, length us, event | category | flops | bytes accessed | tf_op | source)
XLA Modules:
  0.0 163.5 jit_solution(11326516651190494492)
XLA Ops:
  0.6 1.3 reshape.44.packing
  2.0 1.4 reshape.46.sending
  3.3 0.0 copy-start.3
  3.3 0.0 copy-start.2
  3.3 85.1 %shard_map.185 = (bf16[4096,512]{1,0:T(8,128)(2,1)}, bf16[512,512]{1,0:T(8,128)(2,1)}) custom-call(bf16[4096,1024]{1,0:T(8,128)(2,1)} %features.1, bf16[1024,512]{1,0:T(8,128)(2,1)} %weight.1, s32[32,128]{1,0:T(8,128)} %reshape.44.packing, s32[32,128]{1,0:T(8,128)} %bitcast.17, s32[4,128]{1,0:T(4,128)} %reshape.46.sending), custom_call_target="tpu_custom_call" | custom-call | flops 40802189312 | bytes 8388608 | tf_op jit(solution)/shard_map/pallas_call | solution.py:182
  88.5 4.0 %all-to-all-start = ((bf16[32,16,512]{2,1,0:T(8,128)(2,1)}), bf16[32,16,512]{2,1,0:T(8,128)(2,1)S(1)}, u32[]{:S(2)}, u32[]{:S(2)}) async-start(bf16[32,16,512]{2,1,0:T(8,128)(2,1)} %bitcast.16), calls=%async_computation | async-start | bytes 1048576 | tf_op jit(solution)/shard_map/all_to_all | solution.py:364
  92.5 0.0 copy-done.3
  92.5 0.1 copy.21
  92.6 0.7 reshape.43.index
  93.2 0.0 copy-done.2
  93.2 0.7 reshape.50.extra
  93.9 14.1 %all-to-all-done = bf16[32,16,512]{2,1,0:T(8,128)(2,1)S(1)} async-done(((bf16[32,16,512]{2,1,0:T(8,128)(2,1)}), bf16[32,16,512]{2,1,0:T(8,128)(2,1)S(1)}, u32[]{:S(2)}, u32[]{:S(2)}) %all-to-all-start) | async-done | bytes 524320 | tf_op jit(solution)/shard_map/all_to_all | solution.py:364
  108.0 0.0 copy-start
  108.0 0.8 copy-done
  108.8 18.5 %shard_map.186 = (bf16[4096,512]{1,0:T(8,128)(2,1)}, bf16[512,512]{1,0:T(8,128)(2,1)}) custom-call(s32[192]{0:T(256)} %reshape.43.index, s32[32]{0:T(128)} %live.2, bf16[4096,512]{1,0:T(8,128)(2,1)} %get-tuple-element.8.hidden, bf16[512,512]{1,0:T(8,128)(2,1)} %bitcast.13, bf16[32,6,128,128]{3,2,1,0:T(8,128)(2,1)} %tiles.2, s32[32,128]{1,0:T(8,128)} %bitcast.18, ...), custom_call_target="tpu_custom_call" | custom-call | flops 7516192768 | bytes 14680064 | tf_op jit(solution)/shard_map/pallas_call | solution.py:320
  127.3 3.0 %all-to-all-start.1 = ((bf16[32,16,512]{2,1,0:T(8,128)(2,1)}), bf16[32,16,512]{2,1,0:T(8,128)(2,1)S(1)}, u32[]{:S(2)}, u32[]{:S(2)}) async-start(bf16[32,16,512]{2,1,0:T(8,128)(2,1)} %bitcast.15), calls=%async_computation.1 | async-start | bytes 1048576 | tf_op jit(solution)/shard_map/all_to_all | solution.py:364
  130.3 0.0 copy-done.4
  130.3 0.1 copy.20
  130.4 0.7 reshape.42.index
  131.0 14.8 %all-to-all-done.1 = bf16[32,16,512]{2,1,0:T(8,128)(2,1)S(1)} async-done(((bf16[32,16,512]{2,1,0:T(8,128)(2,1)}), bf16[32,16,512]{2,1,0:T(8,128)(2,1)S(1)}, u32[]{:S(2)}, u32[]{:S(2)}) %all-to-all-start.1) | async-done | bytes 524320 | tf_op jit(solution)/shard_map/all_to_all | solution.py:364
  145.8 0.0 copy-done.5
  145.8 0.6 broadcast_in_dim.2.extra
  146.5 0.2 copy-done.1
  146.6 16.9 %shard_map.187 = (bf16[4096,512]{1,0:T(8,128)(2,1)}, f32[8,1,512]{2,1,0:T(1,128)}) custom-call(s32[192]{0:T(256)} %reshape.42.index, s32[32]{0:T(128)} %live.3, bf16[4096,512]{1,0:T(8,128)(2,1)} %get-tuple-element.10.hidden, bf16[512,512]{1,0:T(8,128)(2,1)} %bitcast.14, bf16[32,6,128,128]{3,2,1,0:T(8,128)(2,1)} %tiles.3, s32[32,128]{1,0:T(8,128)} %bitcast.19, ...), custom_call_target="tpu_custom_call" | custom-call | flops 7516192768 | bytes 14680064 | tf_op jit(solution)/shard_map/pallas_call | solution.py:320
  (3 shorter events, 0.0 us)
Async XLA Ops:
  3.3 89.1 %copy-start.3 = (s32[32,6]{0,1:T(8,128)S(1)}, s32[32,6]{0,1:T(8,128)}, u32[]{:S(2)}) copy-start(s32[32,6]{0,1:T(8,128)} %param.24) | copy-start | bytes 2308
  3.3 89.9 %copy-start.2 = (s32[1,1,4,8,16]{4,3,2,1,0:T(8,128)S(1)}, s32[1,1,4,8,16]{4,3,2,1,0:T(8,128)}, u32[]{:S(2)}) copy-start(s32[1,1,4,8,16]{4,3,2,1,0:T(8,128)} %param.23) | copy-start | bytes 6148
  88.5 19.5 %all-to-all-start = ((bf16[32,16,512]{2,1,0:T(8,128)(2,1)}), bf16[32,16,512]{2,1,0:T(8,128)(2,1)S(1)}, u32[]{:S(2)}, u32[]{:S(2)}) async-start(bf16[32,16,512]{2,1,0:T(8,128)(2,1)} %bitcast.16), calls=%async_computation | async-start | bytes 1048576 | tf_op jit(solution)/shard_map/all_to_all | solution.py:364
  108.0 0.8 copy-start
  108.8 21.5 %copy-start.4 = (s32[32,6]{0,1:T(8,128)S(1)}, s32[32,6]{0,1:T(8,128)}, u32[]{:S(2)}) copy-start(s32[32,6]{0,1:T(8,128)} %param.25) | copy-start | bytes 2308
  108.8 37.1 %copy-start.5 = (bf16[512]{0:T(512)(128)(2,1)S(1)}, bf16[512]{0:T(512)(128)(2,1)}, u32[]{:S(2)}) copy-start(bf16[512]{0:T(512)(128)(2,1)} %param.35) | copy-start | bytes 3076
  127.3 18.6 %all-to-all-start.1 = ((bf16[32,16,512]{2,1,0:T(8,128)(2,1)}), bf16[32,16,512]{2,1,0:T(8,128)(2,1)S(1)}, u32[]{:S(2)}, u32[]{:S(2)}) async-start(bf16[32,16,512]{2,1,0:T(8,128)(2,1)} %bitcast.15), calls=%async_computation.1 | async-start | bytes 1048576 | tf_op jit(solution)/shard_map/all_to_all | solution.py:364
  145.8 0.8 copy-start.1

commit v2 on v1

--- a/solution.py
+++ b/solution.py
@@ -13,15 +13,14 @@
 MESH = pl.DeviceIdType.MESH
 
 
-def across(ref, ids, rows):
-    def body(r, carry):
-        row = ref[pl.ds(r, 1), :]
-        wide = jnp.broadcast_to(row, (LANES, LANES)).T
-        lane = lax.broadcasted_iota(jnp.int32, (LANES, LANES), 1)
-        ids[pl.ds(pl.multiple_of(r * LANES, LANES), LANES), :] = wide - lane
-        return carry
-
-    lax.fori_loop(0, rows // LANES, body, 0)
+def across(ref, ids):
+    lines, columns = ref.shape
+    lane = lax.broadcasted_iota(jnp.int32, (LANES, LANES), 1)
+    for r in range(lines):
+        for c in range(columns // LANES):
+            row = ref[r : r + 1, c * LANES : (c + 1) * LANES]
+            first = r * columns + c * LANES
+            ids[first : first + LANES, :] = jnp.broadcast_to(row, (LANES, LANES)).T - lane
 
 
 def one_hot(ids, first, count):
@@ -102,9 +101,9 @@
         return carry
 
     lax.fori_loop(1, n, greet, 0)
-    across(packing, pack_ids, rows)
-    across(placing, place_ids, rows)
-    across(sending, send_ids, outgoing.shape[0])
+    across(packing, pack_ids)
+    across(placing, place_ids)
+    across(sending, send_ids)
 
     def encode(c, carry):
         chunk(c).wait()
@@ -210,18 +209,20 @@
     )(
         features,
         weight,
-        packing.reshape(-1, LANES),
-        placing.reshape(-1, LANES),
+        packing.reshape(n, cap),
+        placing.reshape(1, -1),
         sending.reshape(-1, LANES),
     )
 
 
 def layer_kernel(
     last,
-    index,
-    live,
+    groups,
+    n,
+    near,
+    far,
     hidden,
-    halo,
+    outgoing,
     tiles,
     degree,
     self_weight,
@@ -230,83 +231,175 @@
     out,
     second,
     sources,
-    aggregate,
+    halo,
+    far_tiles,
+    near_sum,
+    self_part,
     ids,
     sem,
+    send_sem,
+    recv_sem,
 ):
     step = pl.program_id(0)
-    rows = hidden.shape[0]
+    count = outgoing.shape[0]
     blocks, slots, size = tiles.shape[:3]
+    span = blocks * size
+    own_blocks = hidden.shape[0]
+    steps = own_blocks // blocks
+    far_blocks = count // size
+    devices = groups * n
+    bound = count // devices
+    me = lax.axis_index("dom") * n + lax.axis_index("shard")
+
+    def device(e):
+        return (e // n, e % n)
+
+    def rows_of(e):
+        return pl.ds(pl.multiple_of(e * bound, bound), bound)
+
+    def transfer(q):
+        to = (me + q) % devices
+        return pltpu.make_async_remote_copy(
+            src_ref=outgoing.at[rows_of(to), :],
+            dst_ref=halo.at[rows_of(me), :],
+            send_sem=send_sem.at[q],
+            recv_sem=recv_sem.at[q],
+            device_id=device(to),
+            device_id_type=MESH,
+        )
+
+    def own_copies():
+        return [
+            pltpu.make_async_copy(hidden, sources.at[pl.ds(0, own_blocks)], sem.at[0]),
+            pltpu.make_async_copy(
+                outgoing.at[rows_of(me), :], halo.at[rows_of(me), :], sem.at[1]
+            ),
+        ]
 
     @pl.when(step == 0)
     def _():
-        own = pltpu.make_async_copy(hidden, sources.at[pl.ds(0, rows), :], sem.at[0])
-        far = pltpu.make_async_copy(halo, sources.at[pl.ds(rows, halo.shape[0]), :], sem.at[1])
-        own.start()
-        far.start()
+        for copy in own_copies():
+            copy.start()
+        barrier = pltpu.get_barrier_semaphore()
+
+        def greet(q, carry):
+            pl.semaphore_signal(
+                barrier, inc=1, device_id=device((me + q) % devices), device_id_type=MESH
+            )
+            return carry
+
+        lax.fori_loop(1, devices, greet, 0)
+        sources[own_blocks] = jnp.zeros_like(sources[own_blocks])
         if not last:
-            across(extra, ids, ids.shape[0])
-        own.wait()
-        far.wait()
-
-    for j in range(blocks):
-        block = step * blocks + j
-        lit = live[block]
-        lhs = jnp.concatenate(
-            [
-                jnp.where(k < lit, tiles[j, k], jnp.zeros((), jnp.bfloat16))
-                for k in range(slots)
-            ],
-            axis=1,
+            across(extra, ids)
+        pl.semaphore_wait(barrier, devices - 1)
+
+        def send(q, carry):
+            transfer(q).start()
+            return carry
+
+        lax.fori_loop(1, devices, send, 0)
+        for copy in own_copies():
+            copy.wait()
+
+    @pl.when(step < steps)
+    def _():
+        for j in range(blocks):
+            block = step * blocks + j
+            first = pl.multiple_of(block * size, size)
+            lhs = jnp.concatenate([tiles[j, k] for k in range(slots)], axis=1)
+            rhs = jnp.concatenate(
+                [sources[near[block * slots + k]] for k in range(slots)], axis=0
+            )
+            near_sum[pl.ds(first, size), :] = dot(lhs, rhs)
+            for f in range(count // size):
+                total = None
+                for k in range(slots):
+                    flag = jnp.full((size, size), far[(block * slots + k) * far_blocks + f])
+                    term = tiles[j, k] * flag.astype(jnp.bfloat16)
+                    total = term if total is None else total + term
+                far_tiles[pl.ds(first, size), f * size : (f + 1) * size] = total
+        here = pl.ds(pl.multiple_of(step * span, span), span)
+        own_rows = sources[pl.ds(step * blocks, blocks)].reshape(span, hidden.shape[2])
+        self_part[here, :] = dot(own_rows, self_weight[...])
+
+    @pl.when(step == steps)
+    def _():
+        def arrive(q, carry):
+            transfer(q).wait_recv()
+            return carry
+
+        lax.fori_loop(1, devices, arrive, 0)
+
+        def leave(q, carry):
+            transfer(q).wait_send()
+            return carry
+
+        lax.fori_loop(1, devices, leave, 0)
+
+    @pl.when(step >= steps)
+    def _():
+        turn = step - steps
+        here = pl.ds(pl.multiple_of(turn * span, span), span)
+        width = out.shape[1]
+        shares = []
+        for j in range(blocks):
+            given = degree[pl.ds(turn * blocks + j, 1), :].astype(jnp.float32)
+            shares.append(1.0 / jnp.broadcast_to(given, (LANES, LANES)).T)
+        share = jnp.concatenate(shares, axis=0)
+        total = near_sum[here, :] + dot(far_tiles[here, :], halo[...])
+        aggregate = (total * jnp.concatenate([share] * (width // LANES), axis=1)).astype(
+            jnp.bfloat16
         )
-        rhs = jnp.concatenate(
-            [
-                sources[pl.ds(pl.multiple_of(index[block * slots + k] * size, size), size), :]
-                for k in range(slots)
-            ],
-            axis=0,
-        )
-        given = degree[pl.ds(block, 1), :].astype(jnp.float32)
-        share = 1.0 / jnp.broadcast_to(given, (LANES, LANES)).T
-        total = dot(lhs, rhs)
-        aggregate[j * size : (j + 1) * size, :] = (
-            total * jnp.concatenate([share] * (total.shape[1] // LANES), axis=1)
-        ).astype(jnp.bfloat16)
-    span = blocks * size
-    own_rows = sources[pl.ds(pl.multiple_of(step * span, span), span), :]
-    mixed = dot(own_rows, self_weight[...]) + dot(aggregate[...], neigh_weight[...])
-    active = jnp.maximum(mixed, 0.0)
-    scale = lax.rsqrt(jnp.mean(active * active, axis=-1, keepdims=True) + 1e-06)
-    result = (active * scale).astype(jnp.bfloat16)
-    out[...] = result
-    if last:
-        logits = lax.dot_general(
-            extra[...], result, (((1,), (1,)), ((), ())), preferred_element_type=jnp.float32
-        )
-        second[...] = jax.nn.sigmoid(logits[0:1, :])[None]
-    else:
-
-        def boundary(r, carry):
-            here = pl.ds(pl.multiple_of(r * STEP, STEP), STEP)
-            found = dot(one_hot(ids[here, :], step * span, span), result).astype(jnp.bfloat16)
-            second[here, :] = jnp.where(step == 0, jnp.zeros_like(found), second[here, :]) + found
-            return carry
-
-        lax.fori_loop(0, second.shape[0] // STEP, boundary, 0)
+        mixed = self_part[here, :] + dot(aggregate, neigh_weight[...])
+        active = jnp.maximum(mixed, 0.0)
+        scale = lax.rsqrt(jnp.mean(active * active, axis=-1, keepdims=True) + 1e-06)
+        result = (active * scale).astype(jnp.bfloat16)
+        out[...] = result
+        if last:
+            logits = lax.dot_general(
+                extra[...], result, (((1,), (1,)), ((), ())), preferred_element_type=jnp.float32
+            )
+            second[...] = jax.nn.sigmoid(logits[0:1, :])[None]
+        else:
+
+            @pl.when(turn == 0)
+            def _():
+                second[...] = jnp.zeros_like(second)
+
+            def boundary(r, carry):
+                part = pl.ds(pl.multiple_of(r * STEP, STEP), STEP)
+                found = dot(one_hot(ids[part, :], turn * span, span), result)
+                second[part, :] = second[part, :] + found.astype(jnp.bfloat16)
+                return carry
+
+            lax.fori_loop(0, second.shape[0] // STEP, boundary, 0)
 
 
 def sage_layer(
-    hidden, halo, tile_index, tile_live, tiles, degree, self_weight, neigh_weight, extra, last
+    hidden, outgoing, tile_index, tile_live, tiles, degree, self_weight, neigh_weight, extra, last
 ):
+    groups, n = lax.axis_size("dom"), lax.axis_size("shard")
     rows, width = hidden.shape
     blocks_all, slots, size = tiles.shape[:3]
     per_step = STEP // size
     steps = blocks_all // per_step
-    count = halo.shape[0]
+    count = outgoing.shape[0]
+
+    used = jnp.where(
+        jnp.arange(slots, dtype=jnp.int32)[None, :] < tile_live[:, None], tile_index, -1
+    )
+    near = jnp.where((used >= 0) & (used < blocks_all), used, blocks_all)
+    far_block = blocks_all + jnp.arange(count // size, dtype=jnp.int32)
+    far = (used[:, :, None] == far_block).astype(jnp.float32)
+
+    def late(i):
+        return (i // steps) * (i - steps)
+
     if last:
         extra = jnp.broadcast_to(extra[None, :], (16, width))
         second_shape = jax.ShapeDtypeStruct((steps, 1, STEP), jnp.float32)
-        second_spec = pl.BlockSpec((1, 1, STEP), lambda i, *_: (i, 0, 0))
+        second_spec = pl.BlockSpec((1, 1, STEP), lambda i, *_: (late(i), 0, 0))
     else:
         extra = extra.reshape(-1, LANES)
         second_shape = jax.ShapeDtypeStruct((extra.size, width), jnp.bfloat16)
@@ -318,56 +411,55 @@
     degree = degree.reshape(-1, LANES)
     any_spec = pl.BlockSpec(memory_space=pl.ANY)
     return pl.pallas_call(
-        functools.partial(layer_kernel, last),
+        functools.partial(layer_kernel, last, groups, n),
         out_shape=(jax.ShapeDtypeStruct((rows, width), jnp.bfloat16), second_shape),
         grid_spec=pltpu.PrefetchScalarGridSpec(
             num_scalar_prefetch=2,
-            grid=(steps,),
+            grid=(2 * steps,),
             in_specs=[
                 any_spec,
                 any_spec,
-                pl.BlockSpec((per_step, slots, size, size), lambda i, *_: (i, 0, 0, 0)),
+                pl.BlockSpec(
+                    (per_step, slots, size, size),
+                    lambda i, *_: (i - (i // steps) * (i - steps + 1), 0, 0, 0),
+                ),
                 whole(degree),
                 whole(self_weight),
                 whole(neigh_weight),
                 whole(extra),
             ],
-            out_specs=(pl.BlockSpec((STEP, width), lambda i, *_: (i, 0)), second_spec),
+            out_specs=(pl.BlockSpec((STEP, width), lambda i, *_: (late(i), 0)), second_spec),
             scratch_shapes=[
-                pltpu.VMEM((rows + count, width), jnp.bfloat16),
-                pltpu.VMEM((STEP, width), jnp.bfloat16),
+                pltpu.VMEM((blocks_all + 1, size, width), jnp.bfloat16),
+                pltpu.VMEM((count, width), jnp.bfloat16),
+                pltpu.VMEM((rows, count), jnp.bfloat16),
+                pltpu.VMEM((rows, width), jnp.float32),
+                pltpu.VMEM((rows, width), jnp.float32),
                 pltpu.VMEM((count, LANES), jnp.int32),
                 pltpu.SemaphoreType.DMA((2,)),
+                pltpu.SemaphoreType.DMA((groups * n,)),
+                pltpu.SemaphoreType.DMA((groups * n,)),
             ],
         ),
-        compiler_params=pltpu.CompilerParams(vmem_limit_bytes=VMEM_LIMIT),
+        compiler_params=pltpu.CompilerParams(
+            collective_id=2 if last else 1, has_side_effects=True, vmem_limit_bytes=VMEM_LIMIT
+        ),
         cost_estimate=pl.CostEstimate(
             flops=2 * rows * width * (slots * size + 2 * width),
             bytes_accessed=tiles.size * 2 + 4 * rows * width,
             transcendentals=0,
         ),
     )(
-        tile_index.reshape(-1),
-        tile_live,
-        hidden,
-        halo,
+        near.reshape(-1),
+        far.reshape(-1),
+        hidden.reshape(blocks_all, size, width),
+        outgoing,
         tiles,
         degree,
         self_weight,
         neigh_weight,
         extra,
     )
-
-
-def exchange(outgoing, devices):
-    width = outgoing.shape[-1]
-    return lax.all_to_all(
-        outgoing.reshape(devices, -1, width),
-        ("dom", "shard"),
-        split_axis=0,
-        concat_axis=0,
-        tiled=True,
-    ).reshape(-1, width)
 
 
 def per_device(
@@ -391,13 +483,12 @@
     head_weight,
 ):
     group_size = lax.axis_size("shard")
-    devices = lax.axis_size("dom") * group_size
     owned, outgoing = relay(
         features, enc_weight, pack_index, place_index, halo_send_one, group_size
     )
     layer_one, outgoing = sage_layer(
         owned,
-        exchange(outgoing, devices),
+        outgoing,
         tile_index_one,
         tile_live_one,
         tiles_one,
@@ -409,7 +500,7 @@
     )
     embedding, probability = sage_layer(
         layer_one,
-        exchange(outgoing, devices),
+        outgoing,
         tile_index_two,
         tile_live_two,
         tiles_two,

time: 164 us -> 152 us (0.927)
  waiting for transfers between devices: 28.9 us -> 0 us
  Pallas kernels: 120 us -> 138 us
  starting transfers between devices: 6.99 us -> 0 us
  local copies, waits for them, and re-layouts: 6.47 us -> 10.8 us
    all_to_all x2 -> x0, waiting for transfers between devices: 28.9 us -> none  [exchange(): lax.all_to_all(outgoing.reshape(devices, -1, width), ('dom', 'shard'), sp...]
    pallas_call x2, Pallas kernels: 35.3 us -> 58.2 us  [sage_layer(): pl.pallas_call(functools.partial(layer_kernel, last, groups, n), out_shap...]
    all_to_all x2 -> x0, starting transfers between devices: 6.99 us -> none  [exchange(): lax.all_to_all(outgoing.reshape(devices, -1, width), ('dom', 'shard'), sp...]
    pallas_call x1, Pallas kernels: 85.1 us -> 79.4 us  [relay(): pl.pallas_call(functools.partial(relay_kernel, n), out_shape=(jax.ShapeDt...]
    unnamed x14 -> x8, local copies, waits for them, and re-layouts: 1.15 us -> 5.09 us
  transfers between devices with their start and end apart: 2 -> 0, of which waited for: 2 -> 0; matrix products, arithmetic and copies ran while one was open for 1% -> 0% of each run, Pallas kernels for 0% -> 0%
where the time goes in v2:
time: 152 us; the launch traced here: 151 us
  Pallas kernels  138 us (91%)
  local copies, waits for them, and re-layouts  10.8 us (7%)
  other arithmetic  1.52 us (1%)
    pallas_call x1, Pallas kernels, relay(): pl.pallas_call(functools.partial(relay_kernel, n), out_shape=(jax.ShapeDt...  79.4 us
    pallas_call x2, Pallas kernels, sage_layer(): pl.pallas_call(functools.partial(layer_kernel, last, groups, n), out_shap...  58.2 us
    unnamed x8, local copies, waits for them, and re-layouts  5.09 us

profile of v2, /device:TPU:0, one launch (start us, length us, event | category | flops | bytes accessed | tf_op | source)
XLA Modules:
  0.0 150.6 jit_solution(1279058473932142944)
XLA Ops:
  0.6 0.7 and_select_fusion.1
  1.3 0.1 copy.22
  1.4 0.6 reshape.56.near
  2.0 0.7 and_select_fusion
  2.7 0.1 copy.25
  2.8 0.1 copy.23
  2.9 0.1 compare_convert_fusion
  3.1 0.7 reshape.66.far
  3.8 0.1 copy.24
  3.8 0.6 reshape.57.near
  4.5 0.7 reshape.67.far
  5.2 1.4 reshape.60.sending
  6.6 0.0 copy-start
  6.6 79.4 %shard_map.185 = (bf16[4096,512]{1,0:T(8,128)(2,1)}, bf16[512,512]{1,0:T(8,128)(2,1)}) custom-call(bf16[4096,1024]{1,0:T(8,128)(2,1)} %features.1, bf16[1024,512]{1,0:T(8,128)(2,1)} %weight.1, s32[8,512]{1,0:T(8,128)} %bitcast.11, s32[1,4096]{1,0:T(1,128)} %bitcast.12, s32[4,128]{1,0:T(4,128)} %reshape.60.sending), custom_call_target="tpu_custom_call" | custom-call | flops 40802189312 | bytes 8388608 | tf_op jit(solution)/shard_map/pallas_call | solution.py:181
  86.0 0.0 copy-done
  86.0 0.7 reshape.63.extra
  86.7 28.4 %shard_map.186 = (bf16[4096,512]{1,0:T(8,128)(2,1)}, bf16[512,512]{1,0:T(8,128)(2,1)}) custom-call(s32[192]{0:T(256)} %reshape.57.near, f32[768]{0:T(1024)} %reshape.67.far, bf16[32,128,512]{2,1,0:T(8,128)(2,1)} %bitcast.16, bf16[512,512]{1,0:T(8,128)(2,1)} %get-tuple-element.9.outgoing, bf16[32,6,128,128]{3,2,1,0:T(8,128)(2,1)} %tiles.2, ...), custom_call_target="tpu_custom_call" | custom-call | flops 7516192768 | bytes 14680064 | tf_op jit(solution)/shard_map/pallas_call | solution.py:413
  115.1 0.0 copy-done.2
  115.1 0.6 broadcast_in_dim.10.extra
  115.7 29.7 %shard_map.187 = (bf16[4096,512]{1,0:T(8,128)(2,1)}, f32[8,1,512]{2,1,0:T(1,128)}) custom-call(s32[192]{0:T(256)} %reshape.56.near, f32[768]{0:T(1024)} %reshape.66.far, bf16[32,128,512]{2,1,0:T(8,128)(2,1)} %bitcast.15, bf16[512,512]{1,0:T(8,128)(2,1)} %get-tuple-element.11.outgoing, bf16[32,6,128,128]{3,2,1,0:T(8,128)(2,1)} %tiles.3, s32[32,128]{1,0:T(8,128)} %bitcast.14, ...), custom_call_target="tpu_custom_call" | custom-call | flops 7516192768 | bytes 14680064 | tf_op jit(solution)/shard_map/pallas_call | solution.py:413
  145.5 0.0 copy-start.1
  145.5 4.5 %copy.28 = bf16[4096,512]{1,0:T(8,128)(2,1)} copy(bf16[4096,512]{1,0:T(8,128)(2,1)} %get-tuple-element.22) | data formatting | bytes 8388608
  150.0 0.0 copy-done.1
  150.0 0.6 copy.29
  (2 shorter events, 0.0 us)
Async XLA Ops:
  6.6 79.5 %copy-start = (s32[1,1,4,8,16]{4,3,2,1,0:T(8,128)S(1)}, s32[1,1,4,8,16]{4,3,2,1,0:T(8,128)}, u32[]{:S(2)}) copy-start(s32[1,1,4,8,16]{4,3,2,1,0:T(8,128)} %param.23) | copy-start | bytes 6148
  86.7 28.4 %copy-start.2 = (bf16[512]{0:T(512)(128)(2,1)S(1)}, bf16[512]{0:T(512)(128)(2,1)}, u32[]{:S(2)}) copy-start(bf16[512]{0:T(512)(128)(2,1)} %param.35) | copy-start | bytes 3076
  145.5 4.5 %copy-start.1 = (f32[8,1,512]{2,1,0:T(1,128)S(1)}, f32[8,1,512]{2,1,0:T(1,128)}, u32[]{:S(2)}) copy-start(f32[8,1,512]{2,1,0:T(1,128)} %get-tuple-element.13) | copy-start | bytes 49156

commit v3 on v2

--- a/solution.py
+++ b/solution.py
@@ -38,7 +38,7 @@
 
 
 def select_rows(ids, table, acc):
-    depth = 2 * STEP
+    depth = 4 * STEP
     acc[...] = jnp.zeros_like(acc)
 
     def body(k, carry):
@@ -137,15 +137,17 @@
     stage[0] = select_rows(ids_for(me), encoded, acc)
 
     def place(source, block, fresh):
+        tall = 2 * STEP
+
         def body(r, carry):
-            here = pl.ds(pl.multiple_of(r * STEP, STEP), STEP)
+            here = pl.ds(pl.multiple_of(r * tall, tall), tall)
             found = dot(one_hot(place_ids[here, :], source * cap, cap), block[...]).astype(
                 jnp.bfloat16
             )
             owned[here, :] = found if fresh else owned[here, :] + found
             return carry
 
-        lax.fori_loop(0, parts, body, 0)
+        lax.fori_loop(0, rows // tall, body, 0)
 
     place(me, stage.at[0], True)
 
@@ -219,8 +221,7 @@
     last,
     groups,
     n,
-    near,
-    far,
+    plan,
     hidden,
     outgoing,
     tiles,
@@ -247,6 +248,8 @@
     own_blocks = hidden.shape[0]
     steps = own_blocks // blocks
     far_blocks = count // size
+    entry = 1 + far_blocks
+    start = own_blocks * slots * entry if last else 0
     devices = groups * n
     bound = count // devices
     me = lax.axis_index("dom") * n + lax.axis_index("shard")
@@ -309,14 +312,14 @@
             first = pl.multiple_of(block * size, size)
             lhs = jnp.concatenate([tiles[j, k] for k in range(slots)], axis=1)
             rhs = jnp.concatenate(
-                [sources[near[block * slots + k]] for k in range(slots)], axis=0
+                [sources[plan[start + (block * slots + k) * entry]] for k in range(slots)], axis=0
             )
             near_sum[pl.ds(first, size), :] = dot(lhs, rhs)
             for f in range(count // size):
                 total = None
                 for k in range(slots):
-                    flag = jnp.full((size, size), far[(block * slots + k) * far_blocks + f])
-                    term = tiles[j, k] * flag.astype(jnp.bfloat16)
+                    flag = plan[start + (block * slots + k) * entry + 1 + f].astype(jnp.float32)
+                    term = tiles[j, k] * jnp.full((size, size), flag).astype(jnp.bfloat16)
                     total = term if total is None else total + term
                 far_tiles[pl.ds(first, size), f * size : (f + 1) * size] = total
         here = pl.ds(pl.multiple_of(step * span, span), span)
@@ -377,7 +380,7 @@
 
 
 def sage_layer(
-    hidden, outgoing, tile_index, tile_live, tiles, degree, self_weight, neigh_weight, extra, last
+    hidden, outgoing, plan, tiles, degree, self_weight, neigh_weight, extra, last
 ):
     groups, n = lax.axis_size("dom"), lax.axis_size("shard")
     rows, width = hidden.shape
@@ -385,13 +388,6 @@
     per_step = STEP // size
     steps = blocks_all // per_step
     count = outgoing.shape[0]
-
-    used = jnp.where(
-        jnp.arange(slots, dtype=jnp.int32)[None, :] < tile_live[:, None], tile_index, -1
-    )
-    near = jnp.where((used >= 0) & (used < blocks_all), used, blocks_all)
-    far_block = blocks_all + jnp.arange(count // size, dtype=jnp.int32)
-    far = (used[:, :, None] == far_block).astype(jnp.float32)
 
     def late(i):
         return (i // steps) * (i - steps)
@@ -414,7 +410,7 @@
         functools.partial(layer_kernel, last, groups, n),
         out_shape=(jax.ShapeDtypeStruct((rows, width), jnp.bfloat16), second_shape),
         grid_spec=pltpu.PrefetchScalarGridSpec(
-            num_scalar_prefetch=2,
+            num_scalar_prefetch=1,
             grid=(2 * steps,),
             in_specs=[
                 any_spec,
@@ -450,8 +446,7 @@
             transcendentals=0,
         ),
     )(
-        near.reshape(-1),
-        far.reshape(-1),
+        plan,
         hidden.reshape(blocks_all, size, width),
         outgoing,
         tiles,
@@ -460,6 +455,16 @@
         neigh_weight,
         extra,
     )
+
+
+def slot_plan(tile_index, tile_live, far_count):
+    blocks, slots = tile_index.shape[1:]
+    on = jnp.arange(slots, dtype=jnp.int32)[None, None, :] < tile_live[:, :, None]
+    used = jnp.where(on, tile_index, -1)[..., None]
+    near = jnp.where((used >= 0) & (used < blocks), used, blocks)
+    part = jnp.arange(1 + far_count, dtype=jnp.int32)
+    flags = (used == blocks - 1 + part).astype(jnp.int32)
+    return jnp.where(part == 0, near, flags).reshape(-1)
 
 
 def per_device(
@@ -483,14 +488,18 @@
     head_weight,
 ):
     group_size = lax.axis_size("shard")
+    plan = slot_plan(
+        jnp.stack([tile_index_one, tile_index_two]),
+        jnp.stack([tile_live_one, tile_live_two]),
+        halo_send_one.size // tiles_one.shape[2],
+    )
     owned, outgoing = relay(
         features, enc_weight, pack_index, place_index, halo_send_one, group_size
     )
     layer_one, outgoing = sage_layer(
         owned,
         outgoing,
-        tile_index_one,
-        tile_live_one,
+        plan,
         tiles_one,
         degree,
         self_weight_one,
@@ -501,8 +510,7 @@
     embedding, probability = sage_layer(
         layer_one,
         outgoing,
-        tile_index_two,
-        tile_live_two,
+        plan,
         tiles_two,
         degree,
         self_weight_two,

time: 152 us -> 146 us (0.961)
  Pallas kernels: 138 us -> 133 us
  local copies, waits for them, and re-layouts: 10.8 us -> 8.72 us
    pallas_call x1, Pallas kernels: 79.4 us -> 75.5 us  [relay(): pl.pallas_call(functools.partial(relay_kernel, n), out_shape=(jax.ShapeDt...]
where the time goes in v3:
time: 146 us; the launch traced here: 144 us
  Pallas kernels  133 us (91%)
  local copies, waits for them, and re-layouts  8.72 us (6%)
  other arithmetic  1.6 us (1%)
    pallas_call x1, Pallas kernels, relay(): pl.pallas_call(functools.partial(relay_kernel, n), out_shape=(jax.ShapeDt...  75.5 us
    pallas_call x2, Pallas kernels, sage_layer(): pl.pallas_call(functools.partial(layer_kernel, last, groups, n), out_shap...  57.9 us
    unnamed x8, local copies, waits for them, and re-layouts  5.09 us

profile of v3, /device:TPU:0, one launch (start us, length us, event | category | flops | bytes accessed | tf_op | source)
XLA Modules:
  0.0 144.4 jit_solution(15012987679316511361)
XLA Ops:
  0.6 0.7 pad_add_fusion
  1.3 0.7 and_select_fusion
  2.0 0.1 copy.22
  2.1 0.1 copy.23
  2.2 0.2 convert_select_fusion
  2.4 0.8 select_n.31.plan
  3.2 1.4 reshape.86.sending
  4.6 0.0 copy-start
  4.6 75.5 %shard_map.185 = (bf16[4096,512]{1,0:T(8,128)(2,1)}, bf16[512,512]{1,0:T(8,128)(2,1)}) custom-call(bf16[4096,1024]{1,0:T(8,128)(2,1)} %features.1, bf16[1024,512]{1,0:T(8,128)(2,1)} %weight.1, s32[8,512]{1,0:T(8,128)} %bitcast.19, s32[1,4096]{1,0:T(1,128)} %bitcast.20, s32[4,128]{1,0:T(4,128)} %reshape.86.sending), custom_call_target="tpu_custom_call" | custom-call | flops 40802189312 | bytes 8388608 | tf_op jit(solution)/shard_map/pallas_call | solution.py:183
  80.1 0.0 copy-done
  80.1 0.7 reshape.89.extra
  80.8 0.0 copy-start.2
  80.8 28.3 %shard_map.186 = (bf16[4096,512]{1,0:T(8,128)(2,1)}, bf16[512,512]{1,0:T(8,128)(2,1)}) custom-call(s32[1920]{0:T(1024)} %select_n.31.plan, bf16[32,128,512]{2,1,0:T(8,128)(2,1)} %bitcast.24, bf16[512,512]{1,0:T(8,128)(2,1)} %get-tuple-element.9.outgoing, bf16[32,6,128,128]{3,2,1,0:T(8,128)(2,1)} %tiles.2, s32[32,128]{1,0:T(8,128)} %bitcast.21, ...), custom_call_target="tpu_custom_call" | custom-call | flops 7516192768 | bytes 14680064 | tf_op jit(solution)/shard_map/pallas_call | solution.py:409
  109.1 0.0 copy-done.2
  109.1 0.6 broadcast_in_dim.31.extra
  109.7 29.6 %shard_map.187 = (bf16[4096,512]{1,0:T(8,128)(2,1)}, f32[8,1,512]{2,1,0:T(1,128)}) custom-call(s32[1920]{0:T(1024)} %select_n.31.plan, bf16[32,128,512]{2,1,0:T(8,128)(2,1)} %bitcast.23, bf16[512,512]{1,0:T(8,128)(2,1)} %get-tuple-element.11.outgoing, bf16[32,6,128,128]{3,2,1,0:T(8,128)(2,1)} %tiles.3, s32[32,128]{1,0:T(8,128)} %bitcast.22, ...), custom_call_target="tpu_custom_call" | custom-call | flops 7516192768 | bytes 14680064 | tf_op jit(solution)/shard_map/pallas_call | solution.py:409
  139.3 0.0 copy-start.1
  139.3 4.5 %copy.26 = bf16[4096,512]{1,0:T(8,128)(2,1)} copy(bf16[4096,512]{1,0:T(8,128)(2,1)} %get-tuple-element.18) | data formatting | bytes 8388608
  143.8 0.0 copy-done.1
  143.8 0.6 copy.27
  (2 shorter events, 0.0 us)
Async XLA Ops:
  4.6 75.5 %copy-start = (s32[1,1,4,8,16]{4,3,2,1,0:T(8,128)S(1)}, s32[1,1,4,8,16]{4,3,2,1,0:T(8,128)}, u32[]{:S(2)}) copy-start(s32[1,1,4,8,16]{4,3,2,1,0:T(8,128)} %param.23) | copy-start | bytes 6148
  80.8 28.3 %copy-start.2 = (bf16[512]{0:T(512)(128)(2,1)S(1)}, bf16[512]{0:T(512)(128)(2,1)}, u32[]{:S(2)}) copy-start(bf16[512]{0:T(512)(128)(2,1)} %param.35) | copy-start | bytes 3076
  139.3 4.5 %copy-start.1 = (f32[8,1,512]{2,1,0:T(1,128)S(1)}, f32[8,1,512]{2,1,0:T(1,128)}, u32[]{:S(2)}) copy-start(f32[8,1,512]{2,1,0:T(1,128)} %get-tuple-element.13) | copy-start | bytes 49156
